TPU v7x, 768 devices: a whole 4x8x12 slice. The times are simulated.
768 devices in a mesh: gx: 8 (over x, core), gy: 96 (over y, z).
Axes of the slice: x: 4, y: 8, z: 12, core: 2. Of those that a mesh axis runs over, the one named last changes fastest.
Arguments:
- chi: float32 [384, 64, 256], P('gy', 'gx'), may hold values from -6 to 6
- sigma: float32 [384, 64, 256], P('gy', 'gx'), may hold values from 25 to 250
- vertical: float32 [4, 64, 64], replicated, may hold values from -0.75 to 0.75
- kx: float32 [384, 64, 256], P('gy', 'gx'), may hold values from 16 to 480
- ky: float32 [384, 64, 256], P('gy', 'gx'), may hold values from 1024 to 30720
Outputs:
- increment: float32 [384, 64, 256], P('gy', 'gx')
All inputs are finite; a program needn't handle non-finite values.
Results may differ from a plain program's by a relative error of at most 0.0003.
Values sent between devices are 32-bit elements; how exact they have to be, the bound alone decides.
No kernel may reach another device: no remote copies, remote signals or barrier semaphores. Data moves between devices by JAX's collectives and lax.ppermute only.
A program may use at most 64 MiB of HBM per device.

v0:
```python
import jax
import jax.numpy as jnp
from jax import lax
from jax.sharding import Mesh
from jax.sharding import PartitionSpec as P

ITERS = 3
GY = ("gy_0", "gy_1")


def from_everyone(value, axis):
    peers = lax.axis_size(axis)
    return lax.all_to_all(
        jnp.broadcast_to(value[None], (peers, *value.shape)), axis, 0, 0, tiled=True
    )


def laid_out(parts, dim):
    dims = list(parts.shape[1:])
    dims[dim] *= parts.shape[0]
    return jnp.moveaxis(parts, 0, dim).reshape(dims)


def gather_directly(value, axis, dim):
    parts = from_everyone(value, axis)
    return laid_out(parts, dim)


def in_blocks(value, dim, peers):
    dims = value.shape
    parts = value.reshape(*dims[:dim], peers, dims[dim] // peers, *dims[dim + 1 :])
    return jnp.moveaxis(parts, dim, 0)


def exchange_in_order(parts, axes, sequence):
    dims = [lax.axis_size(a) for a in axes]
    parts = parts.reshape(*dims, *parts.shape[1:])
    for k in sequence:
        parts = lax.all_to_all(parts, axes[k], split_axis=k, concat_axis=k, tiled=True)
    return parts.reshape(-1, *parts.shape[len(axes) :])


def one_axis_at_a_time(value, axes, sequence, split_dim, concat_dim):
    parts = in_blocks(value, split_dim, lax.axis_size(axes))
    return laid_out(exchange_in_order(parts, axes, sequence), concat_dim)


def mobius_join(earlier, later):
    top_left = later[0] * earlier[0] + later[1] * earlier[2]
    top_right = later[0] * earlier[1] + later[1] * earlier[3]
    low_left = later[2] * earlier[0] + later[3] * earlier[2]
    low_right = later[2] * earlier[1] + later[3] * earlier[3]
    factor = 1.0 / (top_left + top_right + low_left + low_right)
    return (top_left * factor, top_right * factor, low_left * factor, low_right * factor)


def affine_join(earlier, later):
    return (earlier[0] * later[0], later[0] * earlier[1] + later[1])


def mobius_value(matrix):
    return (matrix[0] + matrix[1]) / (matrix[2] + matrix[3])


def neutral(sample):
    filled = jnp.ones_like(sample[0])
    emptied = jnp.zeros_like(sample[0])
    if len(sample) == 4:
        return (filled, emptied, emptied, filled)
    return (filled, emptied)


def settle(gathered, split, join, position):
    ups = tuple((gathered[:, member_id] for member_id in range(split)))
    downs = tuple((gathered[:, member_id] for member_id in range(split, gathered.shape[1])))
    up_scan = lax.associative_scan(join, ups, axis=0)
    down_scan = lax.associative_scan(join, downs, reverse=True, axis=0)
    up_open = neutral(tuple((member[0] for member in ups)))
    down_open = neutral(tuple((member[0] for member in downs)))
    up_in = tuple(
        (
            lax.dynamic_index_in_dim(jnp.concatenate([anchor[None], member], 0), position, 0, False)
            for anchor, member in zip(up_open, up_scan)
        )
    )
    down_in = tuple(
        (
            lax.dynamic_index_in_dim(
                jnp.concatenate([member, anchor[None]], 0), position + 1, 0, False
            )
            for anchor, member in zip(down_open, down_scan)
        )
    )
    return (up_in, down_in)


def across_x(up_total, down_total, join):
    packed = jnp.stack(up_total + down_total, 0)[None]
    gathered = gather_directly(packed, "gx", 0)
    return settle(gathered, len(up_total), join, lax.axis_index("gx"))


def across_y(up_total, down_total, join):
    up_in = neutral(up_total)
    down_in = neutral(down_total)
    return (up_in, down_in)


def chain(up_elements, down_elements, join, axis_dim, across):
    span = up_elements[0].shape[axis_dim]
    up_local = lax.associative_scan(join, up_elements, axis=axis_dim)
    down_local = lax.associative_scan(join, down_elements, reverse=True, axis=axis_dim)
    up_total = tuple((lax.index_in_dim(member, span - 1, axis_dim, False) for member in up_local))
    down_total = tuple((lax.index_in_dim(member, 0, axis_dim, False) for member in down_local))
    up_in, down_in = across(up_total, down_total, join)
    up_whole = join(tuple((jnp.expand_dims(member, axis_dim) for member in up_in)), up_local)
    down_whole = join(tuple((jnp.expand_dims(member, axis_dim) for member in down_in)), down_local)
    return (up_in, up_whole, down_in, down_whole)


def open_edge(conduct, axis_dim, position):
    span = conduct.shape[axis_dim]
    place = lax.broadcasted_iota(jnp.int32, conduct.shape, axis_dim) + position * span
    return jnp.where(place == 0, jnp.zeros_like(conduct), conduct)


def operator_terms(kleft, axis_dim, across):
    span = kleft.shape[axis_dim]
    matrices = (1.0 + kleft, kleft, jnp.ones_like(kleft), kleft)
    up_in, up_whole, down_in, down_whole = chain(matrices, matrices, mobius_join, axis_dim, across)
    after = mobius_value(up_whole)
    before = jnp.concatenate(
        [
            jnp.expand_dims(mobius_value(up_in), axis_dim),
            lax.slice_in_dim(after, 0, span - 1, 1, axis_dim),
        ],
        axis_dim,
    )
    behind_whole = mobius_value(down_whole)
    behind = jnp.concatenate(
        [
            lax.slice_in_dim(behind_whole, 1, span, 1, axis_dim),
            jnp.expand_dims(mobius_value(down_in), axis_dim),
        ],
        axis_dim,
    )
    return (kleft / (before + kleft), kleft / (behind + kleft), after + behind - 1.0)


def line_solve(values, terms, axis_dim, across):
    forward_rate, backward_rate, diagonal = terms
    span = values.shape[axis_dim]
    up_in, up_whole, down_in, down_whole = chain(
        (forward_rate, values),
        (backward_rate, backward_rate * values),
        affine_join,
        axis_dim,
        across,
    )
    passed = down_whole[1]
    passed_next = jnp.concatenate(
        [lax.slice_in_dim(passed, 1, span, 1, axis_dim), jnp.expand_dims(down_in[1], axis_dim)],
        axis_dim,
    )
    return (up_whole[1] + passed_next) / diagonal


def to_lines(field, partners):
    row_count = field.shape[0]
    flattened = field.reshape(row_count, -1)
    padding = -flattened.shape[1] % partners
    return jnp.pad(flattened, ((0, 0), (0, padding)))


def from_lines(lines, target_shape):
    return lines[:, : target_shape[1] * target_shape[2]].reshape(target_shape)


def body(chi, sigma, vertical, kx, ky):
    fields = vertical.shape[0]
    levels = vertical.shape[1]
    width = fields * levels
    scaled = sigma * chi
    blocks = (
        jnp.eye(fields, dtype=jnp.float32)[:, None, :, None] * vertical[:, :, None, :]
    ).reshape(width, width)
    mixed = jnp.dot(scaled.reshape(-1, width), blocks, precision=lax.Precision.HIGHEST).reshape(
        scaled.shape
    )
    x_terms = operator_terms(open_edge(kx, 1, lax.axis_index("gx")), 1, across_x)
    partners = lax.axis_size(GY)
    whole_conduct = lax.all_to_all(
        to_lines(ky, partners), GY, split_axis=1, concat_axis=0, tiled=True
    )
    y_terms = operator_terms(open_edge(whole_conduct, 0, 0), 0, across_y)
    current = mixed
    for sweep in range(ITERS):
        current = line_solve(current, x_terms, 1, across_x)
        whole_lines = one_axis_at_a_time(to_lines(current, partners), GY, (0, 1), 1, 0)
        solved = line_solve(whole_lines, y_terms, 0, across_y)
        current = from_lines(
            lax.all_to_all(solved, GY, split_axis=0, concat_axis=1, tiled=True), current.shape
        )
    return current


def solution(mesh):
    torus = Mesh(mesh.devices.reshape(mesh.shape["gx"], 8, 12), ("gx", "gy_0", "gy_1"))
    in_specs = (P(GY, "gx", None), P(GY, "gx", None), P(), P(GY, "gx", None), P(GY, "gx", None))
    out_specs = P(GY, "gx", None)
    return jax.shard_map(body, mesh=torus, in_specs=in_specs, out_specs=out_specs, check_vma=False)
```

profile of v0, /device:TPU:8, one launch (start us, length us, event | category | flops | bytes accessed | tf_op | source)
XLA Modules:
  0.0 297.9 jit_solution(12564295680691080495)
XLA Ops:
  0.0 0.8 copy.213
  1.0 0.8 copy.165
  1.8 21.9 %all-to-all-start = ((f32[4,96,22]{2,0,1:T(4,128)}), f32[4,96,22]{2,0,1:T(4,128)S(1)}, u32[]{:S(2)}, u32[]{:S(2)}) async-start(f32[4,96,22]{2,0,1:T(4,128)} %copy.165), calls=%async_computation | async-start | bytes 393216 | tf_op jit(solution)/shard_map/all_to_all | solution.py:192
  25.8 0.6 add.3711
  26.6 0.6 add.3712
  27.6 0.6 rev.113
  29.3 11.3 %all-to-all-done = f32[4,96,22]{2,0,1:T(4,128)S(1)} async-done(((f32[4,96,22]{2,0,1:T(4,128)}), f32[4,96,22]{2,0,1:T(4,128)S(1)}, u32[]{:S(2)}, u32[]{:S(2)}) %all-to-all-start) | async-done | bytes 33824 | tf_op jit(solution)/shard_map/all_to_all | solution.py:192
  40.6 0.7 broadcast_in_dim.17
  41.3 4.5 %all-to-all-start.1 = ((f32[8,1,8,4,256]{4,3,2,1,0:T(4,128)}), f32[8,1,8,4,256]{4,3,2,1,0:T(4,128)S(1)}, u32[]{:S(2)}, u32[]{:S(2)}) async-start(f32[8,1,8,4,256]{4,3,2,1,0:T(4,128)} %broadcast_in_dim.17), calls=%async_computation.1 | async-start | bytes 524288 | tf_op jit(solution)/shard_map/all_to_all | solution.py:13
  56.4 0.7 add_multiply_fusion.22
  57.2 0.7 slice-done
  58.1 0.7 pad_maximum_fusion.3
  60.0 0.6 copy-done.60
  60.6 0.7 copy-done.59
  62.7 0.6 copy-done.56
  65.2 0.6 add.3585
  65.9 0.7 fusion.134
  66.8 0.9 copy-done.8
  67.8 0.9 copy-done.6
  73.5 0.6 copy-done.36
  74.3 0.7 copy-done.38
  77.3 0.7 copy-done.48
  81.1 0.7 broadcast_in_dim.18
  81.8 4.8 %all-to-all-start.2 = ((f32[8,1,4,4,256]{4,3,2,1,0:T(4,128)}), f32[8,1,4,4,256]{4,3,2,1,0:T(4,128)S(1)}, u32[]{:S(2)}, u32[]{:S(2)}) async-start(f32[8,1,4,4,256]{4,3,2,1,0:T(4,128)} %broadcast_in_dim.18), calls=%async_computation.2 | async-start | bytes 262144 | tf_op jit(solution)/shard_map/all_to_all | solution.py:13
  86.6 0.9 copy-done.5
  87.9 4.8 %all-to-all-done.2 = f32[8,1,4,4,256]{4,3,2,1,0:T(4,128)S(1)} async-done(((f32[8,1,4,4,256]{4,3,2,1,0:T(4,128)}), f32[8,1,4,4,256]{4,3,2,1,0:T(4,128)S(1)}, u32[]{:S(2)}, u32[]{:S(2)}) %all-to-all-start.2) | async-done | bytes 131104 | tf_op jit(solution)/shard_map/all_to_all | solution.py:13
  93.9 0.9 reshape.236
  94.7 4.2 %all-to-all-start.3 = ((f32[8,1,1056]{2,1,0:T(1,128)}), f32[8,1,1056]{2,1,0:T(1,128)S(1)}, u32[]{:S(2)}, u32[]{:S(2)}) async-start(f32[8,1,1056]{2,1,0:T(1,128)} %reshape.236), calls=%async_computation.3 | async-start | bytes 73728 | tf_op jit(solution)/shard_map/all_to_all | solution.py:39
  99.0 0.9 copy-done.7
  100.1 5.5 %all-to-all-done.3 = f32[8,1,1056]{2,1,0:T(1,128)S(1)} async-done(((f32[8,1,1056]{2,1,0:T(1,128)}), f32[8,1,1056]{2,1,0:T(1,128)S(1)}, u32[]{:S(2)}, u32[]{:S(2)}) %all-to-all-start.3) | async-done | bytes 33824 | tf_op jit(solution)/shard_map/all_to_all | solution.py:39
  106.2 0.7 reduce
  107.2 0.9 reshape.238
  108.0 3.5 %all-to-all-start.4 = ((f32[12,1,704]{2,1,0:T(1,128)}), f32[12,1,704]{2,1,0:T(1,128)S(1)}, u32[]{:S(2)}, u32[]{:S(2)}) async-start(f32[12,1,704]{2,1,0:T(1,128)} %reshape.238), calls=%async_computation.4 | async-start | bytes 73728 | tf_op jit(solution)/shard_map/all_to_all | solution.py:39
  111.7 10.5 %all-to-all-done.4 = f32[12,1,704]{2,1,0:T(1,128)S(1)} async-done(((f32[12,1,704]{2,1,0:T(1,128)}), f32[12,1,704]{2,1,0:T(1,128)S(1)}, u32[]{:S(2)}, u32[]{:S(2)}) %all-to-all-start.4) | async-done | bytes 33824 | tf_op jit(solution)/shard_map/all_to_all | solution.py:39
  122.2 0.7 reduce.1
  129.7 21.2 %all_to_all.126 = f32[96,4,22]{2,1,0:T(4,128)S(1)} all-to-all(f32[96,4,22]{2,1,0:T(4,128)S(1)} %bitcast.351), channel_id=1, replica_groups=mesh['gx'=8,'gy_0'=8,'gy_1'=12] {'gy_0','gy_1'}, dimensions={0} | all-to-all | bytes 67584 | tf_op jit(solution)/shard_map/all_to_all | solution.py:202
  152.5 0.7 broadcast_in_dim.20
  153.1 3.4 %all-to-all-start.6 = ((f32[8,1,4,4,256]{4,3,2,1,0:T(4,128)}), f32[8,1,4,4,256]{4,3,2,1,0:T(4,128)S(1)}, u32[]{:S(2)}, u32[]{:S(2)}) async-start(f32[8,1,4,4,256]{4,3,2,1,0:T(4,128)} %broadcast_in_dim.20), calls=%async_computation.6 | async-start | bytes 262144 | tf_op jit(solution)/shard_map/all_to_all | solution.py:13
  156.6 5.9 %all-to-all-done.6 = f32[8,1,4,4,256]{4,3,2,1,0:T(4,128)S(1)} async-done(((f32[8,1,4,4,256]{4,3,2,1,0:T(4,128)}), f32[8,1,4,4,256]{4,3,2,1,0:T(4,128)S(1)}, u32[]{:S(2)}, u32[]{:S(2)}) %all-to-all-start.6) | async-done | bytes 131104 | tf_op jit(solution)/shard_map/all_to_all | solution.py:13
  164.0 10.7 %all_to_all.127 = f32[8,1,1056]{2,1,0:T(1,128)S(1)} all-to-all(f32[8,1,1056]{2,1,0:T(1,128)S(1)} %reshape.240), channel_id=1, replica_groups=mesh['gx'=8,'gy_0'=8,'gy_1'=12] {'gy_0'}, dimensions={0} | all-to-all | bytes 67584 | tf_op jit(solution)/shard_map/all_to_all | solution.py:39
  174.6 0.7 reduce.2
  175.9 14.0 %all_to_all.128 = f32[12,1,704]{2,1,0:T(1,128)S(1)} all-to-all(f32[12,1,704]{2,1,0:T(1,128)S(1)} %reshape.242), channel_id=1, replica_groups=mesh['gx'=8,'gy_0'=8,'gy_1'=12] {'gy_1'}, dimensions={0} | all-to-all | bytes 67584 | tf_op jit(solution)/shard_map/all_to_all | solution.py:39
  189.9 0.7 reduce.3
  194.1 0.7 slice-done.23
  196.1 0.6 slice-done.11
  199.2 0.6 slice-done.20
  199.8 0.7 slice-done.16
  200.6 0.6 slice-done.12
  201.3 0.6 slice-done.8
  202.9 21.3 %all_to_all.129 = f32[96,4,22]{2,1,0:T(4,128)S(1)} all-to-all(f32[96,4,22]{2,1,0:T(4,128)S(1)} %bitcast.352), channel_id=1, replica_groups=mesh['gx'=8,'gy_0'=8,'gy_1'=12] {'gy_0','gy_1'}, dimensions={0} | all-to-all | bytes 67584 | tf_op jit(solution)/shard_map/all_to_all | solution.py:202
  225.7 0.7 broadcast_in_dim.22
  226.4 3.4 %all-to-all-start.10 = ((f32[8,1,4,4,256]{4,3,2,1,0:T(4,128)}), f32[8,1,4,4,256]{4,3,2,1,0:T(4,128)S(1)}, u32[]{:S(2)}, u32[]{:S(2)}) async-start(f32[8,1,4,4,256]{4,3,2,1,0:T(4,128)} %broadcast_in_dim.22), calls=%async_computation.10 | async-start | bytes 262144 | tf_op jit(solution)/shard_map/all_to_all | solution.py:13
  229.9 5.9 %all-to-all-done.10 = f32[8,1,4,4,256]{4,3,2,1,0:T(4,128)S(1)} async-done(((f32[8,1,4,4,256]{4,3,2,1,0:T(4,128)}), f32[8,1,4,4,256]{4,3,2,1,0:T(4,128)S(1)}, u32[]{:S(2)}, u32[]{:S(2)}) %all-to-all-start.10) | async-done | bytes 131104 | tf_op jit(solution)/shard_map/all_to_all | solution.py:13
  237.3 10.6 %all_to_all.130 = f32[8,1,1056]{2,1,0:T(1,128)S(1)} all-to-all(f32[8,1,1056]{2,1,0:T(1,128)S(1)} %reshape.244), channel_id=1, replica_groups=mesh['gx'=8,'gy_0'=8,'gy_1'=12] {'gy_0'}, dimensions={0} | all-to-all | bytes 67584 | tf_op jit(solution)/shard_map/all_to_all | solution.py:39
  247.9 0.7 reduce.4
  249.1 13.6 %all_to_all.131 = f32[12,1,704]{2,1,0:T(1,128)S(1)} all-to-all(f32[12,1,704]{2,1,0:T(1,128)S(1)} %reshape.246), channel_id=1, replica_groups=mesh['gx'=8,'gy_0'=8,'gy_1'=12] {'gy_1'}, dimensions={0} | all-to-all | bytes 67584 | tf_op jit(solution)/shard_map/all_to_all | solution.py:39
  262.7 0.7 reduce.5
  266.9 0.7 slice-done.21
  268.9 0.6 slice-done.9
  272.6 0.7 slice-done.14
  273.3 0.6 slice-done.10
  274.0 0.6 slice-done.6
  275.6 21.3 %all_to_all.132 = f32[96,4,22]{2,1,0:T(4,128)S(1)} all-to-all(f32[96,4,22]{2,1,0:T(4,128)S(1)} %bitcast.350), channel_id=1, replica_groups=mesh['gx'=8,'gy_0'=8,'gy_1'=12] {'gy_0','gy_1'}, dimensions={0} | all-to-all | bytes 67584 | tf_op jit(solution)/shard_map/all_to_all | solution.py:202
  297.1 0.6 copy.244
  (1851 shorter events, 55.8 us)
Async XLA Ops:
  1.8 21.9 %copy-start.50 = (f32[4,8,256]{2,1,0:T(8,128)S(1)}, f32[4,8,256]{2,1,0:T(8,128)}, u32[]{:S(2)}) copy-start(f32[4,8,256]{2,1,0:T(8,128)} %param.8) | copy-start | bytes 98308
  1.8 38.8 %all-to-all-start = ((f32[4,96,22]{2,0,1:T(4,128)}), f32[4,96,22]{2,0,1:T(4,128)S(1)}, u32[]{:S(2)}, u32[]{:S(2)}) async-start(f32[4,96,22]{2,0,1:T(4,128)} %copy.165), calls=%async_computation | async-start | bytes 393216 | tf_op jit(solution)/shard_map/all_to_all | solution.py:192
  24.8 1.0 copy-start.19
  24.9 0.9 copy-start.21
  24.9 1.5 copy-start.23
  25.0 1.4 copy-start.25
  25.1 1.4 copy-start.27
  25.1 1.3 copy-start.29
  25.2 1.3 copy-start.31
  25.2 1.3 copy-start.33
  27.5 1.3 copy-start.35
  41.3 27.5 %all-to-all-start.1 = ((f32[8,1,8,4,256]{4,3,2,1,0:T(4,128)}), f32[8,1,8,4,256]{4,3,2,1,0:T(4,128)S(1)}, u32[]{:S(2)}, u32[]{:S(2)}) async-start(f32[8,1,8,4,256]{4,3,2,1,0:T(4,128)} %broadcast_in_dim.17), calls=%async_computation.1 | async-start | bytes 524288 | tf_op jit(solution)/shard_map/all_to_all | solution.py:13
  46.2 2.4 copy-start
  57.2 0.7 slice-start
  60.6 0.7 copy-start.59
  66.8 0.9 copy-start.8
  67.7 0.9 copy-start.6
  73.4 0.8 copy-start.36
  73.4 0.8 copy-start.37
  73.5 0.8 copy-start.14
  74.2 0.8 copy-start.38
  74.2 0.8 copy-start.39
  76.3 0.8 copy-start.32
  76.3 0.8 copy-start.34
  76.3 0.8 copy-start.22
  76.3 0.8 copy-start.24
  76.3 0.8 copy-start.26
  76.3 0.8 copy-start.28
  76.4 0.8 copy-start.30
  76.4 0.8 copy-start.20
  77.3 0.8 copy-start.48
  77.3 0.8 copy-start.49
  81.8 10.9 %all-to-all-start.2 = ((f32[8,1,4,4,256]{4,3,2,1,0:T(4,128)}), f32[8,1,4,4,256]{4,3,2,1,0:T(4,128)S(1)}, u32[]{:S(2)}, u32[]{:S(2)}) async-start(f32[8,1,4,4,256]{4,3,2,1,0:T(4,128)} %broadcast_in_dim.18), calls=%async_computation.2 | async-start | bytes 262144 | tf_op jit(solution)/shard_map/all_to_all | solution.py:13
  86.6 0.9 copy-start.5
  94.7 10.9 %all-to-all-start.3 = ((f32[8,1,1056]{2,1,0:T(1,128)}), f32[8,1,1056]{2,1,0:T(1,128)S(1)}, u32[]{:S(2)}, u32[]{:S(2)}) async-start(f32[8,1,1056]{2,1,0:T(1,128)} %reshape.236), calls=%async_computation.3 | async-start | bytes 73728 | tf_op jit(solution)/shard_map/all_to_all | solution.py:39
  99.0 0.9 copy-start.7
  108.0 14.2 %all-to-all-start.4 = ((f32[12,1,704]{2,1,0:T(1,128)}), f32[12,1,704]{2,1,0:T(1,128)S(1)}, u32[]{:S(2)}, u32[]{:S(2)}) async-start(f32[12,1,704]{2,1,0:T(1,128)} %reshape.238), calls=%async_computation.4 | async-start | bytes 73728 | tf_op jit(solution)/shard_map/all_to_all | solution.py:39
  153.1 9.4 %all-to-all-start.6 = ((f32[8,1,4,4,256]{4,3,2,1,0:T(4,128)}), f32[8,1,4,4,256]{4,3,2,1,0:T(4,128)S(1)}, u32[]{:S(2)}, u32[]{:S(2)}) async-start(f32[8,1,4,4,256]{4,3,2,1,0:T(4,128)} %broadcast_in_dim.20), calls=%async_computation.6 | async-start | bytes 262144 | tf_op jit(solution)/shard_map/all_to_all | solution.py:13
  191.6 1.0 copy-start.3
  191.6 0.9 copy-start.11
  191.7 0.8 copy-start.17
  191.8 0.7 copy-start.42
  192.7 1.0 copy-start.4
  192.8 0.9 copy-start.12
  192.9 0.8 copy-start.18
  192.9 0.7 copy-start.43
  194.1 0.7 slice-start.23
  196.1 0.7 slice-start.11
  199.8 0.7 slice-start.16
  200.5 0.7 slice-start.12
  201.2 0.7 slice-start.8
  226.4 9.4 %all-to-all-start.10 = ((f32[8,1,4,4,256]{4,3,2,1,0:T(4,128)}), f32[8,1,4,4,256]{4,3,2,1,0:T(4,128)S(1)}, u32[]{:S(2)}, u32[]{:S(2)}) async-start(f32[8,1,4,4,256]{4,3,2,1,0:T(4,128)} %broadcast_in_dim.22), calls=%async_computation.10 | async-start | bytes 262144 | tf_op jit(solution)/shard_map/all_to_all | solution.py:13
  264.3 1.0 copy-start.1
  264.4 0.9 copy-start.9
  264.5 0.8 copy-start.15
  264.6 0.7 copy-start.40
  265.5 1.0 copy-start.2
  265.6 0.9 copy-start.10
  265.6 0.8 copy-start.16
  265.7 0.7 copy-start.41
  266.8 0.7 slice-start.21
  272.6 0.7 slice-start.14
  273.3 0.7 slice-start.10
  274.0 0.7 slice-start.6
  (30 other events, 18.5 us)
where the time goes:
time: 303 us; the launch traced here: 298 us
  blocking collectives  113 us (37%)
  local copies, waits for them, and re-layouts  68.8 us (23%)
  starting transfers between devices  45.7 us (15%)
  waiting for transfers between devices  43.9 us (14%)
  other arithmetic  17.3 us (6%)
  between operations  9.27 us (3%)
    all_to_all x3, blocking collectives, body(): lax.all_to_all(solved, GY, split_axis=0, concat_axis=1, tiled=True)  63.7 us
    all_to_all x4, blocking collectives, exchange_in_order(): lax.all_to_all(parts, axes[k], split_axis=k, concat_axis=k, tiled=True)  48.9 us
    all_to_all x1, starting transfers between devices, body(): lax.all_to_all(to_lines(ky, partners), GY, split_axis=1, concat_axis=0, t...  21.9 us
    unnamed x151, local copies, waits for them, and re-layouts  18.6 us
    all_to_all x4, waiting for transfers between devices, from_everyone(): lax.all_to_all(jnp.broadcast_to(value[None], (peers, *value.shape)), axis...  16.7 us
    all_to_all x4, starting transfers between devices, from_everyone(): lax.all_to_all(jnp.broadcast_to(value[None], (peers, *value.shape)), axis...  16 us
    all_to_all x2, waiting for transfers between devices, exchange_in_order(): lax.all_to_all(parts, axes[k], split_axis=k, concat_axis=k, tiled=True)  16 us
    slice x279, local copies, waits for them, and re-layouts, chain(): lax.associative_scan(join, down_elements, reverse=True, axis=axis_dim)  16 us
  transfers between devices with their start and end apart: 7, of which 6 were waited for; matrix products, arithmetic and copies ran while one was open for 7% of the time, Pallas kernels for 0%

commit v1 on v0

v1 whole, which is shorter than its diff:
```python
import jax
import jax.numpy as jnp
from jax import lax
from jax.experimental import pallas as pl
from jax.experimental.pallas import tpu as pltpu
from jax.sharding import PartitionSpec as P

ROWS = 4
SPAN = 8
PEERS_X = 8
PEERS_Y = 96
LANES = 128
SLOTS = 3
PAIRS = SLOTS * ROWS
HELD = 16
SUMS = 5

f32 = jnp.float32


def spin(value, shift, axis):
    return pltpu.roll(value, shift % value.shape[axis], axis)


def place(value, axis):
    return lax.broadcasted_iota(jnp.int32, value.shape, axis)


def cell(conduct):
    resist = 1.0 / conduct
    one = jnp.ones_like(conduct)
    return (1.0 + resist, one, resist, one)


def joined(later, earlier):
    a2, b2, c2, k2 = later
    a1, b1, c1, k1 = earlier
    scale = 1.0 / (c2 * b1 + 1.0)
    b = (a2 * b1 + b2) * scale
    c = (c2 * a1 + c1) * scale
    k = k1 * k2 * scale
    return (k * k + b * c, b, c, k)


def kept_where(test, port):
    return tuple(jnp.where(test, m, n) for m, n in zip(port, (1.0, 0.0, 0.0, 1.0)))


def prefixes(port, axis, shifts):
    where = place(port[0], axis)
    for s in shifts:
        earlier = kept_where(where >= s, tuple(spin(m, s, axis) for m in port))
        port = joined(port, earlier)
    return port


def suffixes(port, axis, shifts):
    where = place(port[0], axis)
    size = port[0].shape[axis]
    for s in shifts:
        later = kept_where(where < size - s, tuple(spin(m, -s, axis) for m in port))
        port = joined(later, port)
    return port


def totals(port, source, axis, shifts):
    where = place(source, axis)
    current, tension = source, jnp.zeros_like(source)
    for s in shifts:
        test = where >= s
        earlier = kept_where(test, tuple(spin(m, s, axis) for m in port))
        before = jnp.where(test, spin(current, s, axis), 0.0)
        strain = jnp.where(test, spin(tension, s, axis), 0.0)
        a, b, c, k = port
        gain = 1.0 / k
        current, tension = (
            (a * before + b * strain) * gain + current,
            (c * before + strain) * gain + tension,
        )
        port = joined(port, earlier)
    return port[1], port[2], port[3], current, tension


def x_terms(conduct, front, back, excess_in, behind_in):
    where = place(conduct, 1)
    fa, fb, fc = front
    ba, bb, bc = back
    excess = (fa * excess_in + fb) / (fc * excess_in + 1.0)
    behind = (behind_in + bb) / (bc * behind_in + ba)
    excess_before = jnp.where(where == 0, excess_in, spin(excess, 1, 1))
    behind_next = jnp.where(where == SPAN - 1, behind_in, spin(behind, -1, 1))
    up = conduct / (excess_before + conduct)
    down = conduct / (1.0 + behind_next + conduct)
    inverse = 1.0 / (excess + behind_next)
    up1 = jnp.where(where == 0, 0.0, up)
    up2 = up1 * spin(up1, 1, 1)
    up4 = up2 * spin(up2, 2, 1)
    down1 = jnp.where(where == SPAN - 1, 0.0, down)
    down2 = down1 * spin(down1, -1, 1)
    down4 = down2 * spin(down2, -2, 1)
    up_all, down_all = up, down
    for s in (1, 2, 4):
        up_all = up_all * jnp.where(where >= s, spin(up_all, s, 1), 1.0)
        down_all = down_all * jnp.where(where < SPAN - s, spin(down_all, -s, 1), 1.0)
    down_next = jnp.where(where == SPAN - 1, 1.0, spin(down_all, -1, 1))
    return (
        up1,
        up2,
        up4,
        down,
        down1,
        down2,
        down4,
        inverse,
        up_all * inverse,
        down_next * inverse,
    )


X_TERMS = 10


def x_sweep(values, terms):
    up1, up2, up4, down, down1, down2, down4, inverse = terms[:8]
    ahead = values
    back = down * values
    for s, up_s, down_s in ((1, up1, down1), (2, up2, down2), (4, up4, down4)):
        ahead = ahead + up_s * spin(ahead, s, 1)
        back = back + down_s * spin(back, -s, 1)
    back_next = jnp.where(place(back, 1) == SPAN - 1, 0.0, spin(back, -1, 1))
    return (ahead + back_next) * inverse, ahead, back


Y_SHIFTS = (1, 2, 4, 8, 16, 32, 64)
Y_TERMS = 5


def y_terms(conducts):
    lane = place(conducts[0], 1)
    block = cell(conducts[0])
    for conduct in conducts[1:]:
        block = joined(cell(conduct), block)
    block = kept_where(lane < PEERS_Y, block)
    ahead = prefixes(block, 1, Y_SHIFTS)
    back = suffixes(block, 1, Y_SHIFTS)
    excess = jnp.where(lane == 0, 0.0, spin(ahead[1], 1, 1))
    behind = jnp.where(lane == LANES - 1, 0.0, spin(back[1] / back[0], -1, 1))
    ups, downs, excesses, behinds = [], [], [], []
    for conduct in conducts:
        up = conduct / (excess + conduct)
        excess = 1.0 + up * excess
        ups.append(up)
        excesses.append(excess)
    for conduct in reversed(conducts):
        down = conduct / (1.0 + behind + conduct)
        behinds.append(behind)
        downs.append(down)
        behind = down * (1.0 + behind)
    downs, behinds = downs[::-1], behinds[::-1]
    inverses = [1.0 / (e + h) for e, h in zip(excesses, behinds)]
    up_all = [ups[0]]
    for up in ups[1:]:
        up_all.append(up_all[-1] * up)
    down_all = [downs[-1]]
    for down in downs[-2::-1]:
        down_all.append(down_all[-1] * down)
    down_all = down_all[::-1]
    into_up = [m * inverse for m, inverse in zip(up_all, inverses)]
    into_down = [m * inverse for m, inverse in zip(down_all[1:] + [1.0], inverses)]
    up_s = jnp.where(lane == 0, 0.0, up_all[-1])
    down_s = jnp.where(lane >= PEERS_Y - 1, 0.0, down_all[0])
    steps = []
    for s in Y_SHIFTS:
        steps.append((up_s, down_s))
        up_s = up_s * spin(up_s, s, 1)
        down_s = down_s * spin(down_s, -s, 1)
    return (ups, downs, inverses, into_up, into_down), steps


def y_solve(values, terms, steps):
    ups, downs, inverses, into_up, into_down = terms
    lane = place(values[0], 1)
    ahead = [values[0]]
    for value, up in zip(values[1:], ups[1:]):
        ahead.append(value + up * ahead[-1])
    back = [downs[-1] * values[-1]]
    for value, down in zip(values[-2::-1], downs[-2::-1]):
        back.append(down * (value + back[-1]))
    back = back[::-1]
    up_in, down_in = ahead[-1], back[0]
    for s, (up_s, down_s) in zip(Y_SHIFTS, steps):
        up_in = up_in + up_s * spin(up_in, s, 1)
        down_in = down_in + down_s * spin(down_in, -s, 1)
    up_in = jnp.where(lane == 0, 0.0, spin(up_in, 1, 1))
    down_in = jnp.where(lane >= PEERS_Y - 1, 0.0, spin(down_in, -1, 1))
    solved = []
    for j in range(ROWS):
        here = ahead[j] + back[j + 1] if j + 1 < ROWS else ahead[j]
        solved.append(here * inverses[j] + into_up[j] * up_in + into_down[j] * down_in)
    return solved


def packed(field, fill):
    low, high = field[:, :LANES], field[:, LANES:]
    lane = place(low, 1)
    rest = jnp.where(lane < 32, spin(low, 32, 1), spin(high, 64, 1))
    rest = jnp.where(lane < 64, rest, fill)
    return jnp.concatenate([low, high, rest, jnp.zeros_like(low)], 0).T


def unpacked(lines):
    turned = lines.T
    low, high, rest = turned[:32], turned[32:64], turned[64:96]
    lane = place(low, 1)
    low = jnp.where(lane < PEERS_Y, low, spin(rest, 96, 1))
    high = jnp.where(lane < PEERS_Y, high, spin(rest, 64, 1))
    return jnp.concatenate([low, high], 1)


def filled(lines):
    return jnp.concatenate([lines, jnp.zeros((LANES - PEERS_Y, LANES), f32)], 0)


def mix_kernel(chi, sigma, vertical, kx, ky, out):
    scaled = (sigma[...] * chi[...]).reshape(ROWS * SPAN, 256)
    blank = jnp.zeros((64, 64), f32)
    halves = []
    for h in range(2):
        weight = jnp.concatenate(
            [
                jnp.concatenate([vertical[2 * h], blank], 1),
                jnp.concatenate([blank, vertical[2 * h + 1]], 1),
            ],
            0,
        )
        halves.append(
            jnp.dot(
                scaled[:, h * LANES : (h + 1) * LANES],
                weight,
                precision=lax.Precision.HIGHEST,
                preferred_element_type=f32,
            )
        )
    mixed = jnp.concatenate(halves, 1)
    out[:, 0:LANES] = packed(mixed, 0.0)[:PEERS_Y]
    out[:, LANES : 2 * LANES] = packed(kx[...].reshape(ROWS * SPAN, 256), 1.0)[:PEERS_Y]
    out[:, 2 * LANES : 3 * LANES] = packed(ky[...].reshape(ROWS * SPAN, 256), 1.0)[:PEERS_Y]


def sum_kernel(lines, u_out, kx_out, ky_out, out, rows):
    fields = []
    for n in range(3):
        turned = filled(lines[:, n * LANES : (n + 1) * LANES]).T[: PAIRS * SPAN]
        field = turned.reshape(SLOTS, ROWS, SPAN, LANES)
        if n:
            field = jnp.where(place(field, 3) < PEERS_Y, field, 1.0)
        fields.append(field)
    u, kx, ky = fields
    u_out[...] = u
    kx_out[...] = kx
    ky_out[...] = ky
    rows[...] = jnp.ones_like(rows)
    for c in range(SLOTS):
        sums = totals(cell(kx[c]), u[c], 1, (1, 2, 4))
        for n, total in enumerate(sums):
            for j in range(ROWS):
                at = n * HELD + c * ROWS + j
                rows[at : at + 1, :] = total[j, SPAN - 1 : SPAN, :]
    for q in range(PEERS_X):
        out[q] = rows[...]


def term_kernel(kx, ky, front_out, back_out, y_out, step_out):
    for c in range(SLOTS):
        port = cell(kx[c])
        front = prefixes(port, 1, (1, 2, 4))
        back = suffixes(port, 1, (1, 2, 4))
        for n in range(3):
            front_out[n, c] = front[n]
            back_out[n, c] = back[n]
        terms, steps = y_terms([ky[c, j] for j in range(ROWS)])
        for n, members in enumerate(terms):
            for j, member in enumerate(members):
                y_out[n, c, j] = member
        for n, (up_s, down_s) in enumerate(steps):
            step_out[n, c, 0] = up_s
            step_out[n, c, 1] = down_s


def spread(rows, c):
    return jnp.stack(
        [
            jnp.broadcast_to(rows[c * ROWS + j : c * ROWS + j + 1, :], (SPAN, LANES))
            for j in range(ROWS)
        ]
    )


def loaded_y(y_ref, step_ref, c):
    terms = [[y_ref[n, c, j] for j in range(ROWS)] for n in range(Y_TERMS)]
    steps = [(step_ref[n, c, 0], step_ref[n, c, 1]) for n in range(len(Y_SHIFTS))]
    return terms, steps


def send(here, out, up_rows, down_rows):
    ups, downs = up_rows[...], down_rows[...]
    for q in range(PEERS_X):
        out[q] = jnp.where(q > here, ups, downs)


def start_next(c, solved, x_c, pre_out, up_rows, down_rows):
    pre, ahead, back = x_sweep(solved, x_c)
    pre_out[c] = pre
    for j in range(ROWS):
        at = c * ROWS + j
        up_rows[at : at + 1, :] = ahead[j, SPAN - 1 : SPAN, :]
        down_rows[at : at + 1, :] = back[j, 0:1, :]


def first_kernel(
    where, got, u, kx, front, back, y_ref, step_ref,
    out, pre_out, x_out, rate_out, e_in, h_in, f_in, g_in,
):
    here = where[0]

    def member(q, n):
        return got[q, n * HELD : (n + 1) * HELD, :]

    excess = flow = jnp.zeros((HELD, LANES), f32)
    for q in range(PEERS_X):
        b, c, k, current, tension = (member(q, n) for n in range(SUMS))
        scale = 1.0 / (c * excess + 1.0)
        after = ((k * k + b * c) * excess + b) * scale
        rate = k * scale
        passed = current - after * tension + rate * flow
        rate_out[q] = rate
        excess = jnp.where(q < here, after, excess)
        flow = jnp.where(q < here, passed, flow)
    e_in[...] = excess
    f_in[...] = flow
    behind = flow = jnp.zeros((HELD, LANES), f32)
    for q in reversed(range(PEERS_X)):
        b, c, k, current, tension = (member(q, n) for n in range(SUMS))
        scale = 1.0 / (c * behind + (k * k + b * c))
        rate = k * scale
        passed = rate * (flow + current + behind * tension)
        after = (behind + b) * scale
        rate_out[q] = jnp.where(q > here, rate, rate_out[q])
        behind = jnp.where(q > here, after, behind)
        flow = jnp.where(q > here, passed, flow)
    h_in[...] = behind
    g_in[...] = flow
    up_rows, down_rows = f_in, g_in
    entries = [(spread(f_in, c), spread(g_in, c)) for c in range(SLOTS)]
    for c in range(SLOTS):
        terms = x_terms(
            kx[c],
            tuple(front[n, c] for n in range(3)),
            tuple(back[n, c] for n in range(3)),
            spread(e_in, c),
            spread(h_in, c),
        )
        for n in range(X_TERMS):
            x_out[n, c] = terms[n]
        pre, _, _ = x_sweep(u[c], terms)
        solved = pre + terms[8] * entries[c][0] + terms[9] * entries[c][1]
        solved = jnp.stack(y_solve([solved[j] for j in range(ROWS)], *loaded_y(y_ref, step_ref, c)))
        start_next(c, solved, terms, pre_out, up_rows, down_rows)
    send(here, out, up_rows, down_rows)


def entered(here, got, rates, f_in, g_in):
    flow = jnp.zeros((HELD, LANES), f32)
    for q in range(PEERS_X - 1):
        flow = jnp.where(q < here, got[q] + rates[q] * flow, flow)
    f_in[...] = flow
    flow = jnp.zeros((HELD, LANES), f32)
    for q in reversed(range(1, PEERS_X)):
        flow = jnp.where(q > here, got[q] + rates[q] * flow, flow)
    g_in[...] = flow


def solved_slot(c, pre, x_ref, y_ref, step_ref, f_in, g_in):
    solved = pre[c] + x_ref[8, c] * spread(f_in, c) + x_ref[9, c] * spread(g_in, c)
    return y_solve([solved[j] for j in range(ROWS)], *loaded_y(y_ref, step_ref, c))


def middle_kernel(
    where, got, pre, x_ref, rates, y_ref, step_ref,
    out, pre_out, f_in, g_in, up_rows, down_rows,
):
    here = where[0]
    entered(here, got, rates, f_in, g_in)
    up_rows[...] = jnp.zeros_like(up_rows)
    down_rows[...] = jnp.zeros_like(down_rows)
    for c in range(SLOTS):
        solved = jnp.stack(solved_slot(c, pre, x_ref, y_ref, step_ref, f_in, g_in))
        start_next(c, solved, [x_ref[n, c] for n in range(X_TERMS)], pre_out, up_rows, down_rows)
    send(here, out, up_rows, down_rows)


def last_kernel(where, got, pre, x_ref, rates, y_ref, step_ref, out, f_in, g_in):
    entered(where[0], got, rates, f_in, g_in)
    rows = []
    for c in range(SLOTS):
        rows += solved_slot(c, pre, x_ref, y_ref, step_ref, f_in, g_in)
    rows.append(jnp.zeros((LANES - PAIRS * SPAN, LANES), f32))
    out[...] = jnp.concatenate(rows, 0).T[:PEERS_Y]


def return_kernel(lines, out):
    out[...] = unpacked(filled(lines[...])).reshape(ROWS, SPAN, 256)


def call(kernel, shapes, args, scratch=(), name=None, scalars=0):
    vmem = pl.BlockSpec(memory_space=pltpu.VMEM)
    smem = pl.BlockSpec(memory_space=pltpu.SMEM)
    outs = [jax.ShapeDtypeStruct(shape, f32) for shape in shapes]
    got = pl.pallas_call(
        kernel,
        out_shape=outs,
        in_specs=[smem] * scalars + [vmem] * (len(args) - scalars),
        out_specs=[vmem] * len(outs),
        scratch_shapes=[pltpu.VMEM(shape, f32) for shape in scratch],
        compiler_params=pltpu.CompilerParams(vmem_limit_bytes=16 << 20),
        name=name,
    )(*args)
    return got[0] if len(outs) == 1 else got


FIELD = (SLOTS, ROWS, SPAN, LANES)
ENTRY = (HELD, LANES)


def swapped(value, axis):
    return lax.all_to_all(value, axis, split_axis=0, concat_axis=0, tiled=True)


def body(chi, sigma, vertical, kx, ky):
    here = lax.axis_index("gx").astype(jnp.int32).reshape(1)
    lines = call(mix_kernel, [(PEERS_Y, 3 * LANES)], (chi, sigma, vertical, kx, ky), name="mix")
    lines = swapped(lines, "gy")
    u, kx, ky, sums = call(
        sum_kernel,
        [FIELD, FIELD, FIELD, (PEERS_X, SUMS * HELD, LANES)],
        (lines,),
        [(SUMS * HELD, LANES)],
        name="sums",
    )
    front, back, y_ref, steps = call(
        term_kernel,
        [(3, *FIELD), (3, *FIELD), (Y_TERMS, *FIELD), (len(Y_SHIFTS), SLOTS, 2, SPAN, LANES)],
        (kx, ky),
        name="terms",
    )
    got = swapped(sums, "gx")
    sent, pre, x_ref, rates = call(
        first_kernel,
        [(PEERS_X, *ENTRY), FIELD, (X_TERMS, *FIELD), (PEERS_X, *ENTRY)],
        (here, got, u, kx, front, back, y_ref, steps),
        [ENTRY] * 4,
        name="first",
        scalars=1,
    )
    got = swapped(sent, "gx")
    sent, pre = call(
        middle_kernel,
        [(PEERS_X, *ENTRY), FIELD],
        (here, got, pre, x_ref, rates, y_ref, steps),
        [ENTRY] * 4,
        name="middle",
        scalars=1,
    )
    got = swapped(sent, "gx")
    lines = call(
        last_kernel,
        [(PEERS_Y, LANES)],
        (here, got, pre, x_ref, rates, y_ref, steps),
        [ENTRY] * 2,
        name="last",
        scalars=1,
    )
    lines = swapped(lines, "gy")
    return call(return_kernel, [(ROWS, SPAN, 256)], (lines,), name="back")


def solution(mesh):
    field = P("gy", "gx", None)
    return jax.shard_map(
        body,
        mesh=mesh,
        in_specs=(field, field, P(), field, field),
        out_specs=field,
        check_vma=False,
    )
```

time: 303 us -> 94.3 us (0.31)
  the two profiles are of different devices: /device:TPU:8 before, /device:TPU:1 now
where the time goes in v1:
time: 94.3 us; the launch traced here: 93.7 us
  blocking collectives  70.8 us (75%)
  starting transfers between devices  7.27 us (8%)
  waiting for transfers between devices  5.75 us (6%)
  Pallas kernels  5.72 us (6%)
  local copies, waits for them, and re-layouts  4.1 us (4%)
    all_to_all x4, blocking collectives, swapped(): return lax.all_to_all(value, axis, split_axis=0, concat_axis=0, tiled=True)  70.8 us
    all_to_all x1, starting transfers between devices, swapped(): return lax.all_to_all(value, axis, split_axis=0, concat_axis=0, tiled=True)  7.27 us
    all_to_all x1, waiting for transfers between devices, swapped(): return lax.all_to_all(value, axis, split_axis=0, concat_axis=0, tiled=True)  5.75 us
    pallas_call x7, Pallas kernels, call(): pl.pallas_call(kernel, out_shape=outs, in_specs=[smem] * scalars + [vmem]...  5.72 us
    unnamed x11, local copies, waits for them, and re-layouts  3.94 us
  transfers between devices with their start and end apart: 1, of which 1 were waited for; matrix products, arithmetic and copies ran while one was open for 0% of the time, Pallas kernels for 1%

profile of v1, /device:TPU:1, one launch (start us, length us, event | category | flops | bytes accessed | tf_op | source)
XLA Modules:
  0.0 93.7 jit_solution(17516760180496995021)
XLA Ops:
  0.0 0.0 copy-start
  0.0 0.9 copy-done
  0.9 0.0 copy-start.1
  0.9 0.8 copy-done.1
  1.7 0.0 copy-start.2
  1.7 0.8 copy-done.2
  2.4 0.0 copy-start.3
  2.4 0.8 copy-done.3
  3.2 0.0 copy-start.4
  3.2 0.8 copy-done.4
  3.9 0.4 mix.1
  4.4 0.2 copy.6
  4.5 36.1 %all_to_all.37 = f32[96,1,384]{2,1,0:T(1,128)S(1)} all-to-all(f32[96,1,384]{2,1,0:T(1,128)S(1)} %copy.6), channel_id=1, replica_groups=mesh['gx'=8,'gy'=96] {'gy'}, dimensions={0} | all-to-all | bytes 294912 | tf_op jit(solution)/shard_map/all_to_all | solution.py:436
  40.6 1.0 %sums.1 = (f32[3,4,8,128]{3,2,1,0:T(8,128)S(1)}, f32[3,4,8,128]{3,2,1,0:T(8,128)S(1)}, f32[3,4,8,128]{3,2,1,0:T(8,128)S(1)}, f32[8,80,128]{2,1,0:T(8,128)}) custom-call(f32[96,384]{1,0:T(8,128)S(1)} %bitcast.10), custom_call_target="tpu_custom_call" | custom-call | tf_op jit(solution)/shard_map/sums/pallas_call | solution.py:419
  41.6 7.3 %all-to-all-start.1 = ((f32[8,80,128]{2,1,0:T(8,128)}), f32[8,80,128]{2,1,0:T(8,128)S(1)}, u32[]{:S(2)}, u32[]{:S(2)}) async-start(f32[8,80,128]{2,1,0:T(8,128)} %get-tuple-element.19), calls=%async_computation.1 | async-start | bytes 655360 | tf_op jit(solution)/shard_map/all_to_all | solution.py:436
  48.9 1.3 %terms.1 = (f32[3,3,4,8,128]{4,3,2,1,0:T(8,128)S(1)}, f32[3,3,4,8,128]{4,3,2,1,0:T(8,128)S(1)}, f32[5,3,4,8,128]{4,3,2,1,0:T(8,128)S(1)}, f32[7,3,2,8,128]{4,3,2,1,0:T(8,128)S(1)}) custom-call(f32[3,4,8,128]{3,2,1,0:T(8,128)S(1)} %get-tuple-element.21.kx, f32[3,4,8,128]{3,2,1,0:T(8,128)S(1)} %get-tuple-element.22.ky), custom_call_target="tpu_custom_call" | custom-call | tf_op jit(solution)/shard_map/terms/pallas_call | solution.py:419
  50.2 5.8 %all-to-all-done.1.got = f32[8,80,128]{2,1,0:T(8,128)S(1)} async-done(((f32[8,80,128]{2,1,0:T(8,128)}), f32[8,80,128]{2,1,0:T(8,128)S(1)}, u32[]{:S(2)}, u32[]{:S(2)}) %all-to-all-start.1) | async-done | bytes 327712 | tf_op jit(solution)/shard_map/all_to_all | solution.py:436
  56.0 0.9 first.1
  56.8 8.3 %all_to_all.38.got = f32[8,16,128]{2,1,0:T(8,128)S(1)} all-to-all(f32[8,16,128]{2,1,0:T(8,128)S(1)} %get-tuple-element.27), channel_id=1, replica_groups=mesh['gx'=8,'gy'=96] {'gx'}, dimensions={0} | all-to-all | bytes 131072 | tf_op jit(solution)/shard_map/all_to_all | solution.py:436
  65.2 0.6 middle.1
  65.8 8.0 %all_to_all.39.got = f32[8,16,128]{2,1,0:T(8,128)S(1)} all-to-all(f32[8,16,128]{2,1,0:T(8,128)S(1)} %get-tuple-element.31), channel_id=1, replica_groups=mesh['gx'=8,'gy'=96] {'gx'}, dimensions={0} | all-to-all | bytes 131072 | tf_op jit(solution)/shard_map/all_to_all | solution.py:436
  73.8 0.7 last.1
  74.5 18.4 %all_to_all.40 = f32[96,1,128]{2,1,0:T(1,128)S(1)} all-to-all(f32[96,1,128]{2,1,0:T(1,128)S(1)} %bitcast.11), channel_id=1, replica_groups=mesh['gx'=8,'gy'=96] {'gy'}, dimensions={0} | all-to-all | bytes 98304 | tf_op jit(solution)/shard_map/all_to_all | solution.py:436
  92.9 0.8 back.1
  (1 shorter events, 0.0 us)
Async XLA Ops:
  0.0 0.9 copy-start
  0.9 0.8 copy-start.1
  1.7 0.8 copy-start.2
  2.4 0.8 copy-start.3
  3.2 0.8 copy-start.4
  41.6 14.4 %all-to-all-start.1 = ((f32[8,80,128]{2,1,0:T(8,128)}), f32[8,80,128]{2,1,0:T(8,128)S(1)}, u32[]{:S(2)}, u32[]{:S(2)}) async-start(f32[8,80,128]{2,1,0:T(8,128)} %get-tuple-element.19), calls=%async_computation.1 | async-start | bytes 655360 | tf_op jit(solution)/shard_map/all_to_all | solution.py:436

commit v2 on v0

v2 whole, which is shorter than its diff:
```python
import jax
import jax.numpy as jnp
from jax import lax
from jax.experimental import pallas as pl
from jax.experimental.pallas import tpu as pltpu
from jax.sharding import PartitionSpec as P

ROWS = 4
SPAN = 8
CELLS = ROWS * SPAN
PEERS_X = 8
PEERS_Y = 96
WIDTH = 256
LANES = 128
SLOTS = 3
PARTS = 3
USED = PARTS * CELLS
SENT = PEERS_Y * USED // LANES
TAIL = PEERS_Y - SENT

f32 = jnp.float32


def spin(value, shift, axis):
    return pltpu.roll(value, shift % value.shape[axis], axis)


def place(value, axis):
    return lax.broadcasted_iota(jnp.int32, value.shape, axis)


def strided(start, count, step):
    return pl.ds(start, count, stride=step)


def cell(conduct):
    resist = 1.0 / conduct
    one = jnp.ones_like(conduct)
    return (1.0 + resist, one, resist, one)


def joined(later, earlier):
    a2, b2, c2, k2 = later
    a1, b1, c1, k1 = earlier
    scale = 1.0 / (c2 * b1 + 1.0)
    b = (a2 * b1 + b2) * scale
    c = (c2 * a1 + c1) * scale
    k = k1 * k2 * scale
    return (k * k + b * c, b, c, k)


def kept_where(test, port):
    return tuple(jnp.where(test, m, n) for m, n in zip(port, (1.0, 0.0, 0.0, 1.0)))


def line_terms(conducts, axis, blocks, shifts):
    where = place(conducts[0], axis)
    size = conducts[0].shape[axis]
    block = cell(conducts[0])
    for conduct in conducts[1:]:
        block = joined(cell(conduct), block)
    if blocks < size:
        block = kept_where(where < blocks, block)
    front = back = block
    for s in shifts:
        earlier = kept_where(where >= s, tuple(spin(m, s, axis) for m in front))
        later = kept_where(where < size - s, tuple(spin(m, -s, axis) for m in back))
        front = joined(front, earlier)
        back = joined(later, back)
    excess = jnp.where(where == 0, 0.0, spin(front[1], 1, axis))
    behind = jnp.where(where >= blocks - 1, 0.0, spin(back[1] / back[0], -1, axis))
    ups, downs, excesses, behinds = [], [], [], []
    for conduct in conducts:
        up = conduct / (excess + conduct)
        excess = 1.0 + up * excess
        ups.append(up)
        excesses.append(excess)
    for conduct in reversed(conducts):
        down = conduct / (1.0 + behind + conduct)
        behinds.append(behind)
        downs.append(down)
        behind = down * (1.0 + behind)
    downs, behinds = downs[::-1], behinds[::-1]
    inverses = [1.0 / (e + h) for e, h in zip(excesses, behinds)]
    up_all = [ups[0]]
    for up in ups[1:]:
        up_all.append(up_all[-1] * up)
    down_all = [downs[-1]]
    for down in downs[-2::-1]:
        down_all.append(down_all[-1] * down)
    down_all = down_all[::-1]
    into_up = [m * inverse for m, inverse in zip(up_all, inverses)]
    into_down = [m * inverse for m, inverse in zip(down_all[1:] + [1.0], inverses)]
    up_s = jnp.where(where == 0, 0.0, up_all[-1])
    down_s = jnp.where(where >= blocks - 1, 0.0, down_all[0])
    steps = []
    for s in shifts:
        steps.append((up_s, down_s))
        up_s = up_s * spin(up_s, s, axis)
        down_s = down_s * spin(down_s, -s, axis)
    return ups, downs, inverses, into_up, into_down, steps


def line_solve(values, terms, axis, blocks, shifts):
    ups, downs, inverses, into_up, into_down, steps = terms
    where = place(values[0], axis)
    ahead = [values[0]]
    for value, up in zip(values[1:], ups[1:]):
        ahead.append(value + up * ahead[-1])
    back = [downs[-1] * values[-1]]
    for value, down in zip(values[-2::-1], downs[-2::-1]):
        back.append(down * (value + back[-1]))
    back = back[::-1]
    up_in, down_in = ahead[-1], back[0]
    for s, (up_s, down_s) in zip(shifts, steps):
        up_in = up_in + up_s * spin(up_in, s, axis)
        down_in = down_in + down_s * spin(down_in, -s, axis)
    up_in = jnp.where(where == 0, 0.0, spin(up_in, 1, axis))
    down_in = jnp.where(where >= blocks - 1, 0.0, spin(down_in, -1, axis))
    solved = []
    for n, value in enumerate(ahead):
        here = value + back[n + 1] if n + 1 < len(back) else value
        solved.append(here * inverses[n] + into_up[n] * up_in + into_down[n] * down_in)
    return solved


X_LINE = (1, PEERS_X, (1, 2, 4))
Y_LINE = (2, PEERS_Y, (1, 2, 4, 8, 16, 32, 64))


def turned(lists):
    return [jnp.stack([m[n] for m in lists]) for n in range(lists[0].shape[0])]


def slots(field, fill):
    low, high = field[:, :LANES], field[:, LANES:]
    lane = place(low, 1)
    rest = jnp.where(lane < 32, spin(low, 32, 1), spin(high, 64, 1))
    return low, high, jnp.where(lane < 64, rest, fill)


def mix_kernel(*refs):
    given, out, (chi, sigma, vertical, kx, ky), done = refs[:5], refs[5], refs[6:11], refs[11]
    copies = [
        pltpu.make_async_copy(source, target, done.at[n])
        for n, (source, target) in enumerate(zip(given, (chi, sigma, vertical, kx, ky)))
    ]
    for copy in copies:
        copy.start()
    for copy in copies:
        copy.wait()
    scaled = (sigma[...] * chi[...]).reshape(CELLS, WIDTH)
    blank = jnp.zeros((64, 64), f32)
    halves = []
    for h in range(2):
        weight = jnp.concatenate(
            [
                jnp.concatenate([vertical[2 * h], blank], 1),
                jnp.concatenate([blank, vertical[2 * h + 1]], 1),
            ],
            0,
        )
        halves.append(
            jnp.dot(
                scaled[:, h * LANES : (h + 1) * LANES],
                weight,
                precision=lax.Precision.HIGHEST,
                preferred_element_type=f32,
            )
        )
    mixed = jnp.concatenate(halves, 1)
    parts = [
        slots(mixed, 0.0),
        slots(kx[...].reshape(CELLS, WIDTH), 1.0),
        slots(ky[...].reshape(CELLS, WIDTH), 1.0),
    ]
    blank = jnp.zeros((CELLS, LANES), f32)
    for c in range(SLOTS):
        block = jnp.concatenate([part[c] for part in parts] + [blank], 0).T
        out[:, c * LANES : (c + 1) * LANES] = block[:PEERS_Y]


def deal_kernel(lines, out):
    blocks = []
    for c in range(SLOTS):
        block = lines[:, c * LANES : (c + 1) * LANES]
        head, tail = block[:SENT], block[SENT:]
        moved = jnp.concatenate([spin(tail, USED - n * CELLS, 1) for n in range(PARTS)], 0)
        blocks.append(jnp.where(place(head, 1) < USED, head, moved))
    for q in range(PEERS_X):
        out[q] = blocks[q % SLOTS]


def dealt(block):
    lane = place(block[:TAIL], 1)
    tail = jnp.zeros((TAIL, LANES), f32)
    for n in reversed(range(PARTS)):
        moved = spin(block[n * TAIL : (n + 1) * TAIL], n * CELLS - USED, 1)
        tail = jnp.where(lane < (n + 1) * CELLS, moved, tail)
    return jnp.concatenate([block, tail], 0)


def solve_kernel(got, out, rows):
    lane = place(jnp.zeros((LANES - PEERS_Y, LANES), f32), 1)
    spare = jnp.where(lane < CELLS, 0.0, 1.0)
    for q in range(PEERS_X):
        block = jnp.concatenate([dealt(got[q]), spare], 0).T
        rows[q * USED : (q + 1) * USED, :] = block[:USED]

    def field(n):
        return [
            [rows[strided(n * CELLS + j * SPAN + i, PEERS_X, USED), :] for j in range(ROWS)]
            for i in range(SPAN)
        ]

    u = [jnp.stack(m) for m in field(0)]
    x_terms = line_terms([jnp.stack(m) for m in field(1)], *X_LINE)
    y_terms = line_terms(turned([jnp.stack(m) for m in field(2)]), *Y_LINE)
    for _ in range(3):
        u = turned(line_solve(u, x_terms, *X_LINE))
        u = turned(line_solve(u, y_terms, *Y_LINE))
    for i in range(SPAN):
        for j in range(ROWS):
            out[strided(j * SPAN + i, PEERS_X, CELLS), :] = u[i][j]


def turn_kernel(got, out):
    blank = jnp.zeros((LANES - SLOTS * CELLS, LANES), f32)
    out[...] = jnp.concatenate([got[c] for c in range(SLOTS)] + [blank], 0).T[:PEERS_Y]


def back_kernel(lines, out):
    blank = jnp.zeros((LANES - PEERS_Y, LANES), f32)
    block = jnp.concatenate([lines[...], blank], 0).T
    low, high, rest = (block[c * CELLS : (c + 1) * CELLS] for c in range(SLOTS))
    lane = place(low, 1)
    low = jnp.where(lane < PEERS_Y, low, spin(rest, 96, 1))
    high = jnp.where(lane < PEERS_Y, high, spin(rest, 64, 1))
    out[...] = jnp.concatenate([low, high], 1).reshape(ROWS, SPAN, WIDTH)


def call(kernel, shape, args, name, scratch=(), space=pltpu.VMEM):
    return pl.pallas_call(
        kernel,
        out_shape=jax.ShapeDtypeStruct(shape, f32),
        in_specs=[pl.BlockSpec(memory_space=space)] * len(args),
        out_specs=pl.BlockSpec(memory_space=pltpu.VMEM),
        scratch_shapes=scratch,
        compiler_params=pltpu.CompilerParams(vmem_limit_bytes=16 << 20),
        name=name,
    )(*args)


def swapped(value, axis):
    return lax.all_to_all(value, axis, split_axis=0, concat_axis=0, tiled=True)


def body(chi, sigma, vertical, kx, ky):
    given = (chi, sigma, vertical, kx, ky)
    given = tuple(pltpu.with_memory_space_constraint(m, pltpu.HBM) for m in given)
    lines = call(
        mix_kernel,
        (PEERS_Y, SLOTS * LANES),
        given,
        "mix",
        [pltpu.VMEM(m.shape, f32) for m in given] + [pltpu.SemaphoreType.DMA((5,))],
        pl.ANY,
    )
    lines = swapped(lines, "gy")
    planes = call(deal_kernel, (PEERS_X, SENT, LANES), (lines,), "deal")
    planes = swapped(planes, "gx")
    planes = call(
        solve_kernel,
        (PEERS_X * CELLS, LANES),
        (planes,),
        "solve",
        [pltpu.VMEM((PEERS_X * USED, LANES), f32)],
    )
    planes = swapped(planes.reshape(PEERS_X, CELLS, LANES), "gx")
    lines = call(turn_kernel, (PEERS_Y, LANES), (planes,), "turn")
    lines = swapped(lines, "gy")
    return call(back_kernel, (ROWS, SPAN, WIDTH), (lines,), "back")


def solution(mesh):
    field = P("gy", "gx", None)
    return jax.shard_map(
        body,
        mesh=mesh,
        in_specs=(field, field, P(), field, field),
        out_specs=field,
        check_vma=False,
    )
```

time: 303 us -> 83.2 us (0.27)
  the two profiles are of different devices: /device:TPU:8 before, /device:TPU:1 now
where the time goes in v2:
time: 83.2 us; the launch traced here: 83 us
  blocking collectives  77 us (93%)
  Pallas kernels  5.72 us (7%)
    all_to_all x4, blocking collectives, swapped(): return lax.all_to_all(value, axis, split_axis=0, concat_axis=0, tiled=True)  77 us
    pallas_call x5, Pallas kernels, call(): pl.pallas_call(kernel, out_shape=jax.ShapeDtypeStruct(shape, f32), in_spe...  5.72 us

profile of v2, /device:TPU:1, one launch (start us, length us, event | category | flops | bytes accessed | tf_op | source)
XLA Modules:
  0.0 83.0 jit_solution(4183578536403999055)
XLA Ops:
  0.0 1.4 %mix.1 = f32[96,384]{1,0:T(8,128)S(1)} custom-call(f32[4,8,256]{2,1,0:T(8,128)} %refs_0_.1, f32[4,8,256]{2,1,0:T(8,128)} %refs_1_.1, f32[4,64,64]{2,1,0:T(8,128)} %refs_2_.1, f32[4,8,256]{2,1,0:T(8,128)} %refs_3_.1, f32[4,8,256]{2,1,0:T(8,128)} %refs_4_.1), custom_call_target="tpu_custom_call" | custom-call | tf_op jit(solution)/shard_map/mix/pallas_call | solution.py:243
  1.4 0.2 copy.6
  1.6 36.1 %all_to_all.32 = f32[96,1,384]{2,1,0:T(1,128)S(1)} all-to-all(f32[96,1,384]{2,1,0:T(1,128)S(1)} %copy.6), channel_id=1, replica_groups=mesh['gx'=8,'gy'=96] {'gy'}, dimensions={0} | all-to-all | bytes 294912 | tf_op jit(solution)/shard_map/all_to_all | solution.py:255
  37.7 0.1 deal.1
  37.8 14.4 %all_to_all.33.got = f32[8,72,128]{2,1,0:T(8,128)S(1)} all-to-all(f32[8,72,128]{2,1,0:T(8,128)S(1)} %deal.1), channel_id=1, replica_groups=mesh['gx'=8,'gy'=96] {'gx'}, dimensions={0} | all-to-all | bytes 589824 | tf_op jit(solution)/shard_map/all_to_all | solution.py:255
  52.1 3.3 %solve.1 = f32[256,128]{1,0:T(8,128)S(1)} custom-call(f32[8,72,128]{2,1,0:T(8,128)S(1)} %all_to_all.33.got), custom_call_target="tpu_custom_call" | custom-call | tf_op jit(solution)/shard_map/solve/pallas_call | solution.py:243
  55.5 8.2 %all_to_all.34.got = f32[8,32,128]{2,1,0:T(8,128)S(1)} all-to-all(f32[8,32,128]{2,1,0:T(8,128)S(1)} %bitcast.11), channel_id=1, replica_groups=mesh['gx'=8,'gy'=96] {'gx'}, dimensions={0} | all-to-all | bytes 262144 | tf_op jit(solution)/shard_map/all_to_all | solution.py:255
  63.7 0.1 turn.1
  63.8 18.4 %all_to_all.35 = f32[96,1,128]{2,1,0:T(1,128)S(1)} all-to-all(f32[96,1,128]{2,1,0:T(1,128)S(1)} %bitcast.13), channel_id=1, replica_groups=mesh['gx'=8,'gy'=96] {'gy'}, dimensions={0} | all-to-all | bytes 98304 | tf_op jit(solution)/shard_map/all_to_all | solution.py:255
  82.2 0.8 back.1
  (1 shorter events, 0.0 us)

commit v3 on v2

--- a/solution.py
+++ b/solution.py
@@ -49,26 +49,43 @@
     return (k * k + b * c, b, c, k)
 
 
-def kept_where(test, port):
-    return tuple(jnp.where(test, m, n) for m, n in zip(port, (1.0, 0.0, 0.0, 1.0)))
+def moved(members, shift, axis, test):
+    return [jnp.where(test, spin(m, shift, axis), n) for m, n in members]
+
+
+def ends(block, axis, shifts):
+    where = place(block[0], axis)
+    size = block[0].shape[axis]
+    front = back = block
+    for s in shifts[:-1]:
+        b, c, k = moved(zip(front[1:], (0.0, 0.0, 1.0)), s, axis, where >= s)
+        front = joined(front, (k * k + b * c, b, c, k))
+        b, c, k = moved(zip(back[1:], (0.0, 0.0, 1.0)), -s, axis, where < size - s)
+        back = joined((k * k + b * c, b, c, k), back)
+    s = shifts[-1]
+    a, b, c, k = front
+    e, rate = moved(((b, 0.0), (k, 1.0)), s, axis, where >= s)
+    scale = 1.0 / (c * e + 1.0)
+    excess, passed_up = (a * e + b) * scale, k * rate * scale
+    a, b, c, k = back
+    scale = 1.0 / a
+    h, rate = moved(((b * scale, 0.0), (k * scale, 1.0)), -s, axis, where < size - s)
+    scale = 1.0 / (c * h + a)
+    return excess, passed_up, (h + b) * scale, k * rate * scale
 
 
 def line_terms(conducts, axis, blocks, shifts):
     where = place(conducts[0], axis)
-    size = conducts[0].shape[axis]
     block = cell(conducts[0])
     for conduct in conducts[1:]:
         block = joined(cell(conduct), block)
-    if blocks < size:
-        block = kept_where(where < blocks, block)
-    front = back = block
-    for s in shifts:
-        earlier = kept_where(where >= s, tuple(spin(m, s, axis) for m in front))
-        later = kept_where(where < size - s, tuple(spin(m, -s, axis) for m in back))
-        front = joined(front, earlier)
-        back = joined(later, back)
-    excess = jnp.where(where == 0, 0.0, spin(front[1], 1, axis))
-    behind = jnp.where(where >= blocks - 1, 0.0, spin(back[1] / back[0], -1, axis))
+    if blocks < conducts[0].shape[axis]:
+        block = tuple(
+            jnp.where(where < blocks, m, n) for m, n in zip(block, (1.0, 0.0, 0.0, 1.0))
+        )
+    excess, passed_up, behind, passed_down = ends(block, axis, shifts)
+    excess = jnp.where(where == 0, 0.0, spin(excess, 1, axis))
+    behind = jnp.where(where >= blocks - 1, 0.0, spin(behind, -1, axis))
     ups, downs, excesses, behinds = [], [], [], []
     for conduct in conducts:
         up = conduct / (excess + conduct)
@@ -91,6 +108,12 @@
     down_all = down_all[::-1]
     into_up = [m * inverse for m, inverse in zip(up_all, inverses)]
     into_down = [m * inverse for m, inverse in zip(down_all[1:] + [1.0], inverses)]
+    if axis == LANE:
+        into_up = [m * spin(passed_up, 1, axis) for m in into_up]
+        into_down = [m * spin(passed_down, -1, axis) for m in into_down]
+        used = where < blocks
+        steps = [jnp.where(used, 1.0 / m, 0.0) for m in (passed_up, passed_down)]
+        return ups, downs, inverses, into_up, into_down, steps
     up_s = jnp.where(where == 0, 0.0, up_all[-1])
     down_s = jnp.where(where >= blocks - 1, 0.0, down_all[0])
     steps = []
@@ -101,7 +124,26 @@
     return ups, downs, inverses, into_up, into_down, steps
 
 
-def line_solve(values, terms, axis, blocks, shifts):
+def earlier_and_later():
+    blank = jnp.zeros((2 * LANES, 2 * LANES), f32)
+    row, column = place(blank, 0), place(blank, 1)
+    ahead = jnp.where(column < LANES, column - row, row - column)
+    return jnp.where(ahead > 0, 1.0, 0.0).astype(jnp.bfloat16)
+
+
+def summed(ups, downs, sums):
+    rows = ups.shape[0] * ups.shape[1]
+    rest = jnp.concatenate([ups.reshape(rows, LANES), downs.reshape(rows, LANES)], 1)
+    pieces = []
+    for _ in range(3):
+        pieces.append(rest.astype(jnp.bfloat16))
+        rest = rest - pieces[-1].astype(f32)
+    got = jnp.dot(jnp.concatenate(pieces, 0), sums, preferred_element_type=f32)
+    got = got[:rows] + (got[rows : 2 * rows] + got[2 * rows :])
+    return got[:, :LANES].reshape(ups.shape), got[:, LANES:].reshape(ups.shape)
+
+
+def line_solve(values, terms, axis, blocks, shifts, sums=None):
     ups, downs, inverses, into_up, into_down, steps = terms
     where = place(values[0], axis)
     ahead = [values[0]]
@@ -112,11 +154,14 @@
         back.append(down * (value + back[-1]))
     back = back[::-1]
     up_in, down_in = ahead[-1], back[0]
-    for s, (up_s, down_s) in zip(shifts, steps):
-        up_in = up_in + up_s * spin(up_in, s, axis)
-        down_in = down_in + down_s * spin(down_in, -s, axis)
-    up_in = jnp.where(where == 0, 0.0, spin(up_in, 1, axis))
-    down_in = jnp.where(where >= blocks - 1, 0.0, spin(down_in, -1, axis))
+    if axis == LANE:
+        up_in, down_in = summed(up_in * steps[0], down_in * steps[1], sums)
+    else:
+        for s, (up_s, down_s) in zip(shifts, steps):
+            up_in = up_in + up_s * spin(up_in, s, axis)
+            down_in = down_in + down_s * spin(down_in, -s, axis)
+        up_in = jnp.where(where == 0, 0.0, spin(up_in, 1, axis))
+        down_in = jnp.where(where >= blocks - 1, 0.0, spin(down_in, -1, axis))
     solved = []
     for n, value in enumerate(ahead):
         here = value + back[n + 1] if n + 1 < len(back) else value
@@ -124,8 +169,9 @@
     return solved
 
 
+LANE = 2
 X_LINE = (1, PEERS_X, (1, 2, 4))
-Y_LINE = (2, PEERS_Y, (1, 2, 4, 8, 16, 32, 64))
+Y_LINE = (LANE, PEERS_Y, (1, 2, 4, 8, 16, 32, 64))
 
 
 def turned(lists):
@@ -205,23 +251,28 @@
     spare = jnp.where(lane < CELLS, 0.0, 1.0)
     for q in range(PEERS_X):
         block = jnp.concatenate([dealt(got[q]), spare], 0).T
-        rows[q * USED : (q + 1) * USED, :] = block[:USED]
+        for n in range(PARTS * ROWS):
+            rows[strided(n * SPAN * PEERS_X + q, SPAN, PEERS_X), :] = block[n * SPAN : (n + 1) * SPAN]
 
     def field(n):
-        return [
-            [rows[strided(n * CELLS + j * SPAN + i, PEERS_X, USED), :] for j in range(ROWS)]
-            for i in range(SPAN)
-        ]
-
+        at = [[((n * ROWS + j) * SPAN + i) * PEERS_X for j in range(ROWS)] for i in range(SPAN)]
+        return [[rows[m : m + PEERS_X, :] for m in some] for some in at]
+
+    sums = earlier_and_later()
     u = [jnp.stack(m) for m in field(0)]
     x_terms = line_terms([jnp.stack(m) for m in field(1)], *X_LINE)
     y_terms = line_terms(turned([jnp.stack(m) for m in field(2)]), *Y_LINE)
     for _ in range(3):
         u = turned(line_solve(u, x_terms, *X_LINE))
-        u = turned(line_solve(u, y_terms, *Y_LINE))
+        u = turned(line_solve(u, y_terms, *Y_LINE, sums))
     for i in range(SPAN):
         for j in range(ROWS):
-            out[strided(j * SPAN + i, PEERS_X, CELLS), :] = u[i][j]
+            at = (j * SPAN + i) * PEERS_X
+            rows[at : at + PEERS_X, :] = u[i][j]
+    for q in range(PEERS_X):
+        for j in range(ROWS):
+            at = q * CELLS + j * SPAN
+            out[at : at + SPAN, :] = rows[strided(j * SPAN * PEERS_X + q, SPAN, PEERS_X), :]
 
 
 def turn_kernel(got, out):

time: 83.2 us -> 81.7 us (0.982)
  Pallas kernels: 5.72 us -> 4.18 us
    pallas_call x5, Pallas kernels: 5.72 us -> 4.18 us  [call(): pl.pallas_call(kernel, out_shape=jax.ShapeDtypeStruct(shape, f32), in_spe...]
where the time goes in v3:
time: 81.7 us; the launch traced here: 81.4 us
  blocking collectives  77 us (94%)
  Pallas kernels  4.18 us (5%)
    all_to_all x4, blocking collectives, swapped(): return lax.all_to_all(value, axis, split_axis=0, concat_axis=0, tiled=True)  77 us
    pallas_call x5, Pallas kernels, call(): pl.pallas_call(kernel, out_shape=jax.ShapeDtypeStruct(shape, f32), in_spe...  4.18 us

profile of v3, /device:TPU:1, one launch (start us, length us, event | category | flops | bytes accessed | tf_op | source)
XLA Modules:
  0.0 81.4 jit_solution(10341177760253660995)
XLA Ops:
  0.0 1.4 %mix.1 = f32[96,384]{1,0:T(8,128)S(1)} custom-call(f32[4,8,256]{2,1,0:T(8,128)} %refs_0_.1, f32[4,8,256]{2,1,0:T(8,128)} %refs_1_.1, f32[4,64,64]{2,1,0:T(8,128)} %refs_2_.1, f32[4,8,256]{2,1,0:T(8,128)} %refs_3_.1, f32[4,8,256]{2,1,0:T(8,128)} %refs_4_.1), custom_call_target="tpu_custom_call" | custom-call | tf_op jit(solution)/shard_map/mix/pallas_call | solution.py:294
  1.4 0.2 copy.6
  1.6 36.1 %all_to_all.32 = f32[96,1,384]{2,1,0:T(1,128)S(1)} all-to-all(f32[96,1,384]{2,1,0:T(1,128)S(1)} %copy.6), channel_id=1, replica_groups=mesh['gx'=8,'gy'=96] {'gy'}, dimensions={0} | all-to-all | bytes 294912 | tf_op jit(solution)/shard_map/all_to_all | solution.py:306
  37.7 0.1 deal.1
  37.8 14.4 %all_to_all.33.got = f32[8,72,128]{2,1,0:T(8,128)S(1)} all-to-all(f32[8,72,128]{2,1,0:T(8,128)S(1)} %deal.1), channel_id=1, replica_groups=mesh['gx'=8,'gy'=96] {'gx'}, dimensions={0} | all-to-all | bytes 589824 | tf_op jit(solution)/shard_map/all_to_all | solution.py:306
  52.1 1.8 %solve.1 = f32[256,128]{1,0:T(8,128)S(1)} custom-call(f32[8,72,128]{2,1,0:T(8,128)S(1)} %all_to_all.33.got), custom_call_target="tpu_custom_call" | custom-call | tf_op jit(solution)/shard_map/solve/pallas_call | solution.py:294
  53.9 8.2 %all_to_all.34.got = f32[8,32,128]{2,1,0:T(8,128)S(1)} all-to-all(f32[8,32,128]{2,1,0:T(8,128)S(1)} %bitcast.11), channel_id=1, replica_groups=mesh['gx'=8,'gy'=96] {'gx'}, dimensions={0} | all-to-all | bytes 262144 | tf_op jit(solution)/shard_map/all_to_all | solution.py:306
  62.1 0.1 turn.1
  62.2 18.4 %all_to_all.35 = f32[96,1,128]{2,1,0:T(1,128)S(1)} all-to-all(f32[96,1,128]{2,1,0:T(1,128)S(1)} %bitcast.13), channel_id=1, replica_groups=mesh['gx'=8,'gy'=96] {'gy'}, dimensions={0} | all-to-all | bytes 98304 | tf_op jit(solution)/shard_map/all_to_all | solution.py:306
  80.6 0.8 back.1
  (1 shorter events, 0.0 us)

commit v4 on v3

--- a/solution.py
+++ b/solution.py
@@ -191,8 +191,8 @@
         pltpu.make_async_copy(source, target, done.at[n])
         for n, (source, target) in enumerate(zip(given, (chi, sigma, vertical, kx, ky)))
     ]
-    for copy in copies:
-        copy.start()
+    for n in (2, 0, 1, 3, 4):
+        copies[n].start()
     for copy in copies:
         copy.wait()
     scaled = (sigma[...] * chi[...]).reshape(CELLS, WIDTH)
@@ -223,13 +223,13 @@
     blank = jnp.zeros((CELLS, LANES), f32)
     for c in range(SLOTS):
         block = jnp.concatenate([part[c] for part in parts] + [blank], 0).T
-        out[:, c * LANES : (c + 1) * LANES] = block[:PEERS_Y]
+        out[strided(c, PEERS_Y, SLOTS), :] = block[:PEERS_Y]
 
 
 def deal_kernel(lines, out):
     blocks = []
     for c in range(SLOTS):
-        block = lines[:, c * LANES : (c + 1) * LANES]
+        block = lines[strided(c, PEERS_Y, SLOTS), :]
         head, tail = block[:SENT], block[SENT:]
         moved = jnp.concatenate([spin(tail, USED - n * CELLS, 1) for n in range(PARTS)], 0)
         blocks.append(jnp.where(place(head, 1) < USED, head, moved))
@@ -269,15 +269,25 @@
         for j in range(ROWS):
             at = (j * SPAN + i) * PEERS_X
             rows[at : at + PEERS_X, :] = u[i][j]
+    lane = place(u[0][0], 1)
     for q in range(PEERS_X):
-        for j in range(ROWS):
-            at = q * CELLS + j * SPAN
-            out[at : at + SPAN, :] = rows[strided(j * SPAN * PEERS_X + q, SPAN, PEERS_X), :]
+        *head, tail = (rows[strided(j * SPAN * PEERS_X + q, SPAN, PEERS_X), :] for j in range(ROWS))
+        for j, value in enumerate(head):
+            moved = spin(tail, USED - j * CELLS, 1)
+            out[q, j * SPAN : (j + 1) * SPAN, :] = jnp.where(lane < USED, value, moved)
 
 
 def turn_kernel(got, out):
     blank = jnp.zeros((LANES - SLOTS * CELLS, LANES), f32)
-    out[...] = jnp.concatenate([got[c] for c in range(SLOTS)] + [blank], 0).T[:PEERS_Y]
+    lane = place(jnp.zeros((SPAN, LANES), f32), 1)
+    blocks = []
+    for c in range(SLOTS):
+        tail = jnp.zeros((SPAN, LANES), f32)
+        for j in reversed(range(PARTS)):
+            moved = spin(got[c, j * SPAN : (j + 1) * SPAN, :], j * CELLS - USED, 1)
+            tail = jnp.where(lane < (j + 1) * CELLS, moved, tail)
+        blocks += [got[c], tail]
+    out[...] = jnp.concatenate(blocks + [blank], 0).T[:PEERS_Y]
 
 
 def back_kernel(lines, out):
@@ -311,23 +321,23 @@
     given = tuple(pltpu.with_memory_space_constraint(m, pltpu.HBM) for m in given)
     lines = call(
         mix_kernel,
-        (PEERS_Y, SLOTS * LANES),
+        (PEERS_Y * SLOTS, LANES),
         given,
         "mix",
         [pltpu.VMEM(m.shape, f32) for m in given] + [pltpu.SemaphoreType.DMA((5,))],
         pl.ANY,
     )
-    lines = swapped(lines, "gy")
+    lines = swapped(lines.reshape(PEERS_Y, 1, SLOTS * LANES), "gy").reshape(lines.shape)
     planes = call(deal_kernel, (PEERS_X, SENT, LANES), (lines,), "deal")
     planes = swapped(planes, "gx")
     planes = call(
         solve_kernel,
-        (PEERS_X * CELLS, LANES),
+        (PEERS_X, CELLS - SPAN, LANES),
         (planes,),
         "solve",
         [pltpu.VMEM((PEERS_X * USED, LANES), f32)],
     )
-    planes = swapped(planes.reshape(PEERS_X, CELLS, LANES), "gx")
+    planes = swapped(planes, "gx")
     lines = call(turn_kernel, (PEERS_Y, LANES), (planes,), "turn")
     lines = swapped(lines, "gy")
     return call(back_kernel, (ROWS, SPAN, WIDTH), (lines,), "back")

time: 81.7 us -> 81.3 us (level)
  no operation moved by 1% of the time
where the time goes in v4:
time: 81.3 us; the launch traced here: 81.1 us
  blocking collectives  76.7 us (94%)
  Pallas kernels  4.29 us (5%)
    all_to_all x4, blocking collectives, swapped(): return lax.all_to_all(value, axis, split_axis=0, concat_axis=0, tiled=True)  76.7 us
    pallas_call x5, Pallas kernels, call(): pl.pallas_call(kernel, out_shape=jax.ShapeDtypeStruct(shape, f32), in_spe...  4.29 us

profile of v4, /device:TPU:1, one launch (start us, length us, event | category | flops | bytes accessed | tf_op | source)
XLA Modules:
  0.0 81.1 jit_solution(3971208663816806104)
XLA Ops:
  0.0 1.4 %mix.1 = f32[288,128]{1,0:T(8,128)S(1)} custom-call(f32[4,8,256]{2,1,0:T(8,128)} %refs_0_.1, f32[4,8,256]{2,1,0:T(8,128)} %refs_1_.1, f32[4,64,64]{2,1,0:T(8,128)} %refs_2_.1, f32[4,8,256]{2,1,0:T(8,128)} %refs_3_.1, f32[4,8,256]{2,1,0:T(8,128)} %refs_4_.1), custom_call_target="tpu_custom_call" | custom-call | tf_op jit(solution)/shard_map/mix/pallas_call | solution.py:304
  1.4 36.1 %all_to_all.26 = f32[96,1,384]{2,1,0:T(1,128)S(1)} all-to-all(f32[96,1,384]{2,1,0:T(1,128)S(1)} %bitcast.7), channel_id=1, replica_groups=mesh['gx'=8,'gy'=96] {'gy'}, dimensions={0} | all-to-all | bytes 294912 | tf_op jit(solution)/shard_map/all_to_all | solution.py:316
  37.5 0.1 deal.1
  37.6 14.4 %all_to_all.27.got = f32[8,72,128]{2,1,0:T(8,128)S(1)} all-to-all(f32[8,72,128]{2,1,0:T(8,128)S(1)} %deal.1), channel_id=1, replica_groups=mesh['gx'=8,'gy'=96] {'gx'}, dimensions={0} | all-to-all | bytes 589824 | tf_op jit(solution)/shard_map/all_to_all | solution.py:316
  51.9 1.9 %solve.1 = f32[8,24,128]{2,1,0:T(8,128)S(1)} custom-call(f32[8,72,128]{2,1,0:T(8,128)S(1)} %all_to_all.27.got), custom_call_target="tpu_custom_call" | custom-call | tf_op jit(solution)/shard_map/solve/pallas_call | solution.py:304
  53.8 7.9 %all_to_all.28.got = f32[8,24,128]{2,1,0:T(8,128)S(1)} all-to-all(f32[8,24,128]{2,1,0:T(8,128)S(1)} %solve.1), channel_id=1, replica_groups=mesh['gx'=8,'gy'=96] {'gx'}, dimensions={0} | all-to-all | bytes 196608 | tf_op jit(solution)/shard_map/all_to_all | solution.py:316
  61.7 0.1 turn.1
  61.9 18.4 %all_to_all.29 = f32[96,1,128]{2,1,0:T(1,128)S(1)} all-to-all(f32[96,1,128]{2,1,0:T(1,128)S(1)} %bitcast.9), channel_id=1, replica_groups=mesh['gx'=8,'gy'=96] {'gy'}, dimensions={0} | all-to-all | bytes 98304 | tf_op jit(solution)/shard_map/all_to_all | solution.py:316
  80.3 0.8 back.1

commit v5 on v4

--- a/solution.py
+++ b/solution.py
@@ -193,7 +193,7 @@
     ]
     for n in (2, 0, 1, 3, 4):
         copies[n].start()
-    for copy in copies:
+    for copy in copies[:3]:
         copy.wait()
     scaled = (sigma[...] * chi[...]).reshape(CELLS, WIDTH)
     blank = jnp.zeros((64, 64), f32)
@@ -215,6 +215,8 @@
             )
         )
     mixed = jnp.concatenate(halves, 1)
+    for copy in copies[3:]:
+        copy.wait()
     parts = [
         slots(mixed, 0.0),
         slots(kx[...].reshape(CELLS, WIDTH), 1.0),
@@ -227,9 +229,10 @@
 
 
 def deal_kernel(lines, out):
+    spare = jnp.zeros((LANES - PEERS_Y, LANES), f32)
     blocks = []
     for c in range(SLOTS):
-        block = lines[strided(c, PEERS_Y, SLOTS), :]
+        block = jnp.concatenate([lines[strided(c, PEERS_Y, SLOTS), :], spare], 0).T[:USED]
         head, tail = block[:SENT], block[SENT:]
         moved = jnp.concatenate([spin(tail, USED - n * CELLS, 1) for n in range(PARTS)], 0)
         blocks.append(jnp.where(place(head, 1) < USED, head, moved))
@@ -247,10 +250,8 @@
 
 
 def solve_kernel(got, out, rows):
-    lane = place(jnp.zeros((LANES - PEERS_Y, LANES), f32), 1)
-    spare = jnp.where(lane < CELLS, 0.0, 1.0)
     for q in range(PEERS_X):
-        block = jnp.concatenate([dealt(got[q]), spare], 0).T
+        block = dealt(got[q])
         for n in range(PARTS * ROWS):
             rows[strided(n * SPAN * PEERS_X + q, SPAN, PEERS_X), :] = block[n * SPAN : (n + 1) * SPAN]
 

time: 81.3 us -> 81.3 us (level)
  no operation moved by 1% of the time
where the time goes in v5:
time: 81.3 us; the launch traced here: 81 us
  blocking collectives  76.7 us (94%)
  Pallas kernels  4.25 us (5%)
    all_to_all x4, blocking collectives, swapped(): return lax.all_to_all(value, axis, split_axis=0, concat_axis=0, tiled=True)  76.7 us
    pallas_call x5, Pallas kernels, call(): pl.pallas_call(kernel, out_shape=jax.ShapeDtypeStruct(shape, f32), in_spe...  4.25 us

profile of v5, /device:TPU:1, one launch (start us, length us, event | category | flops | bytes accessed | tf_op | source)
XLA Modules:
  0.0 81.0 jit_solution(11764515345953501265)
XLA Ops:
  0.0 1.4 %mix.1 = f32[288,128]{1,0:T(8,128)S(1)} custom-call(f32[4,8,256]{2,1,0:T(8,128)} %refs_0_.1, f32[4,8,256]{2,1,0:T(8,128)} %refs_1_.1, f32[4,64,64]{2,1,0:T(8,128)} %refs_2_.1, f32[4,8,256]{2,1,0:T(8,128)} %refs_3_.1, f32[4,8,256]{2,1,0:T(8,128)} %refs_4_.1), custom_call_target="tpu_custom_call" | custom-call | tf_op jit(solution)/shard_map/mix/pallas_call | solution.py:305
  1.4 36.1 %all_to_all.26 = f32[96,1,384]{2,1,0:T(1,128)S(1)} all-to-all(f32[96,1,384]{2,1,0:T(1,128)S(1)} %bitcast.7), channel_id=1, replica_groups=mesh['gx'=8,'gy'=96] {'gy'}, dimensions={0} | all-to-all | bytes 294912 | tf_op jit(solution)/shard_map/all_to_all | solution.py:317
  37.5 0.2 deal.1
  37.7 14.4 %all_to_all.27.got = f32[8,72,128]{2,1,0:T(8,128)S(1)} all-to-all(f32[8,72,128]{2,1,0:T(8,128)S(1)} %deal.1), channel_id=1, replica_groups=mesh['gx'=8,'gy'=96] {'gx'}, dimensions={0} | all-to-all | bytes 589824 | tf_op jit(solution)/shard_map/all_to_all | solution.py:317
  52.0 1.7 %solve.1 = f32[8,24,128]{2,1,0:T(8,128)S(1)} custom-call(f32[8,72,128]{2,1,0:T(8,128)S(1)} %all_to_all.27.got), custom_call_target="tpu_custom_call" | custom-call | tf_op jit(solution)/shard_map/solve/pallas_call | solution.py:305
  53.8 7.9 %all_to_all.28.got = f32[8,24,128]{2,1,0:T(8,128)S(1)} all-to-all(f32[8,24,128]{2,1,0:T(8,128)S(1)} %solve.1), channel_id=1, replica_groups=mesh['gx'=8,'gy'=96] {'gx'}, dimensions={0} | all-to-all | bytes 196608 | tf_op jit(solution)/shard_map/all_to_all | solution.py:317
  61.7 0.1 turn.1
  61.8 18.4 %all_to_all.29 = f32[96,1,128]{2,1,0:T(1,128)S(1)} all-to-all(f32[96,1,128]{2,1,0:T(1,128)S(1)} %bitcast.9), channel_id=1, replica_groups=mesh['gx'=8,'gy'=96] {'gy'}, dimensions={0} | all-to-all | bytes 98304 | tf_op jit(solution)/shard_map/all_to_all | solution.py:317
  80.2 0.8 back.1

commit v6 on v5

--- a/solution.py
+++ b/solution.py
@@ -37,6 +37,14 @@
     resist = 1.0 / conduct
     one = jnp.ones_like(conduct)
     return (1.0 + resist, one, resist, one)
+
+
+def lengthened(conduct, earlier):
+    a, b, c, k = earlier
+    scale = 1.0 / (b + conduct)
+    share = conduct * scale
+    b, c, k = 1.0 + share * b, a * scale + share * c, share * k
+    return (k * k + b * c, b, c, k)
 
 
 def joined(later, earlier):
@@ -78,7 +86,7 @@
     where = place(conducts[0], axis)
     block = cell(conducts[0])
     for conduct in conducts[1:]:
-        block = joined(cell(conduct), block)
+        block = lengthened(conduct, block)
     if blocks < conducts[0].shape[axis]:
         block = tuple(
             jnp.where(where < blocks, m, n) for m, n in zip(block, (1.0, 0.0, 0.0, 1.0))

time: 81.3 us -> 81.3 us (level)
  no operation moved by 1% of the time
where the time goes in v6:
time: 81.3 us; the launch traced here: 81.1 us
  blocking collectives  76.7 us (94%)
  Pallas kernels  4.28 us (5%)
    all_to_all x4, blocking collectives, swapped(): return lax.all_to_all(value, axis, split_axis=0, concat_axis=0, tiled=True)  76.7 us
    pallas_call x5, Pallas kernels, call(): pl.pallas_call(kernel, out_shape=jax.ShapeDtypeStruct(shape, f32), in_spe...  4.28 us

profile of v6, /device:TPU:1, one launch (start us, length us, event | category | flops | bytes accessed | tf_op | source)
XLA Modules:
  0.0 81.1 jit_solution(12725748586138187403)
XLA Ops:
  0.0 1.4 %mix.1 = f32[288,128]{1,0:T(8,128)S(1)} custom-call(f32[4,8,256]{2,1,0:T(8,128)} %refs_0_.1, f32[4,8,256]{2,1,0:T(8,128)} %refs_1_.1, f32[4,64,64]{2,1,0:T(8,128)} %refs_2_.1, f32[4,8,256]{2,1,0:T(8,128)} %refs_3_.1, f32[4,8,256]{2,1,0:T(8,128)} %refs_4_.1), custom_call_target="tpu_custom_call" | custom-call | tf_op jit(solution)/shard_map/mix/pallas_call | solution.py:313
  1.4 36.1 %all_to_all.26 = f32[96,1,384]{2,1,0:T(1,128)S(1)} all-to-all(f32[96,1,384]{2,1,0:T(1,128)S(1)} %bitcast.7), channel_id=1, replica_groups=mesh['gx'=8,'gy'=96] {'gy'}, dimensions={0} | all-to-all | bytes 294912 | tf_op jit(solution)/shard_map/all_to_all | solution.py:325
  37.5 0.2 deal.1
  37.7 14.4 %all_to_all.27.got = f32[8,72,128]{2,1,0:T(8,128)S(1)} all-to-all(f32[8,72,128]{2,1,0:T(8,128)S(1)} %deal.1), channel_id=1, replica_groups=mesh['gx'=8,'gy'=96] {'gx'}, dimensions={0} | all-to-all | bytes 589824 | tf_op jit(solution)/shard_map/all_to_all | solution.py:325
  52.0 1.8 %solve.1 = f32[8,24,128]{2,1,0:T(8,128)S(1)} custom-call(f32[8,72,128]{2,1,0:T(8,128)S(1)} %all_to_all.27.got), custom_call_target="tpu_custom_call" | custom-call | tf_op jit(solution)/shard_map/solve/pallas_call | solution.py:313
  53.8 7.9 %all_to_all.28.got = f32[8,24,128]{2,1,0:T(8,128)S(1)} all-to-all(f32[8,24,128]{2,1,0:T(8,128)S(1)} %solve.1), channel_id=1, replica_groups=mesh['gx'=8,'gy'=96] {'gx'}, dimensions={0} | all-to-all | bytes 196608 | tf_op jit(solution)/shard_map/all_to_all | solution.py:325
  61.7 0.1 turn.1
  61.9 18.4 %all_to_all.29 = f32[96,1,128]{2,1,0:T(1,128)S(1)} all-to-all(f32[96,1,128]{2,1,0:T(1,128)S(1)} %bitcast.9), channel_id=1, replica_groups=mesh['gx'=8,'gy'=96] {'gy'}, dimensions={0} | all-to-all | bytes 98304 | tf_op jit(solution)/shard_map/all_to_all | solution.py:325
  80.3 0.8 back.1
